TPU v7x, 32 devices: a whole 2x2x4 slice. The times are simulated.
32 devices in a mesh: guide: 2 (over core), tensor: 2 (over y), batch: 8 (over z, x).
Axes of the slice: x: 2, y: 2, z: 4, core: 2. Of those that a mesh axis runs over, the one named last changes fastest.
Arguments:
- latents: float32 [8, 16, 448], P('batch'), may hold values from -6 to 6
- lengths: int32 [8], P('batch'), may hold values from 1 to 448, 2240 in all
- timesteps: int32 [8], P('batch'), may hold values from 100 to 599
- guidance: float32 [8], P('batch'), may hold values from 1.5 to 6
- condition: float32 [2, 8, 1152], P('guide', 'batch'), may hold values from -6 to 6
- embed_weight: float32 [16, 1152], replicated, may hold values from -1.5 to 1.5
- modulation_weight: bfloat16 [2, 1152, 6, 1152], P(None, 'batch', None, 'tensor'), may hold values from -0.1875 to 0.1875
- final_modulation: bfloat16 [1152, 2, 1152], P('batch', None, 'tensor'), may hold values from -0.1875 to 0.1875
- qkv_weight: bfloat16 [2, 1152, 3, 1152], P(None, 'batch', None, 'tensor'), may hold values from -15 to 15
- proj_weight: bfloat16 [2, 1152, 1152], P(None, 'tensor', 'batch'), may hold values from -0.1875 to 0.1875
- up_weight: bfloat16 [2, 1152, 4608], P(None, 'batch', 'tensor'), may hold values from -0.1875 to 0.1875
- down_weight: bfloat16 [2, 4608, 1152], P(None, 'tensor', 'batch'), may hold values from -0.09375 to 0.09375
- output_weight: bfloat16 [1152, 16], replicated, may hold values from -0.1875 to 0.1875
Outputs:
- guided_noise: float32 [8, 16, 448], P('batch', 'guide', 'tensor')
- previous_latents: float32 [8, 16, 448], P('batch', 'guide', 'tensor')
Inputs may be any that keep to these rules, and one draw needn't show every extreme that they name: `lengths`: at least one request has exactly 448 live tokens; all requests together have 8 * 448 * 5 // 8.
All inputs are finite; a program needn't handle non-finite values. No bound on the sum of `lengths` on one device may be relied on, other than what follows from the above.
Results may differ from a plain program's by a relative error of at most 0.025.
Values may be sent and summed in bfloat16 or wider, within the bound.
No kernel may reach another device: no remote copies, remote signals or barrier semaphores. Data moves between devices by JAX's collectives and lax.ppermute only.
A program may use at most 128 MiB of HBM per device.

v0:
```python
import math
import jax
import jax.numpy as jnp
from jax import lax
from jax.sharding import PartitionSpec as P

HDIM = 72
TRAIN_STEPS = 1000
STRIDE = 20
norm_epsilon = 1e-06


def from_partner(block, axis, distance):
    count = lax.axis_size(axis)
    route = []
    for low in range(count):
        high = low | 1 << distance
        if high != low and high < count:
            route += [(low, high), (high, low)]
    return lax.ppermute(block, axis, route)


def layer_norm(values):
    center = values - jnp.mean(values, axis=-1, keepdims=True)
    spread = jnp.mean(center * center, axis=-1, keepdims=True)
    return center * lax.rsqrt(spread + norm_epsilon)


def modulate(values, shift, scale):
    return layer_norm(values) * (1.0 + scale[:, None, :]) + shift[:, None, :]


def position_table(row_count, width):
    rows_at = jnp.arange(row_count, dtype=jnp.int32).astype(jnp.float32)
    half_width = width // 2
    frequency = jnp.exp(
        jnp.arange(half_width, dtype=jnp.float32) * (-math.log(10000.0) / half_width)
    )
    angles = rows_at[:, None] * frequency[None, :]
    return jnp.concatenate([jnp.sin(angles), jnp.cos(angles)], axis=1)


def attend(operands):
    projected_item, key_live = operands
    score_scale = 1.0 / math.sqrt(HDIM)
    scores = (
        jnp.einsum(
            "qhd,khd->hqk",
            projected_item[:, 0],
            projected_item[:, 1],
            preferred_element_type=jnp.float32,
        )
        * score_scale
    )
    scores = jnp.where(key_live[None, None, :], scores, -jnp.inf)
    row_max = jnp.max(scores, axis=-1, keepdims=True)
    exp_scores = jnp.exp(scores - row_max)
    probabilities = (exp_scores / jnp.sum(exp_scores, axis=-1, keepdims=True)).astype(jnp.bfloat16)
    attended = jnp.einsum(
        "hqk,khd->qhd", probabilities, projected_item[:, 2], preferred_element_type=jnp.float32
    )
    return attended.astype(jnp.bfloat16).reshape(
        attended.shape[0], attended.shape[1] * attended.shape[2]
    )


def local(
    latents,
    lengths,
    timesteps,
    guidance,
    condition,
    embed_weight,
    modulation_weight,
    final_modulation,
    qkv_weight,
    proj_weight,
    up_weight,
    down_weight,
    output_weight,
):
    tensor_count = lax.axis_size("tensor")
    batch_count = lax.axis_size("batch")
    tensor_at = lax.axis_index("tensor")
    batch_at = lax.axis_index("batch")
    guide_at = lax.axis_index("guide")
    req_local, patch_size, max_len = latents.shape
    width = embed_weight.shape[1]
    layer_count = qkv_weight.shape[0]
    head_cols = qkv_weight.shape[3]
    heads_local = head_cols // HDIM
    rows_local = max_len // tensor_count
    width_piece = width // batch_count
    mod_count = 6 * layer_count + 2
    is_first = guide_at == 0

    def rows_product(activation, shard):
        return jnp.dot(
            activation,
            lax.all_gather(shard, "batch", axis=0, tiled=True),
            preferred_element_type=jnp.float32,
        )

    def cols_product(activation, shard):
        return jnp.dot(
            activation,
            lax.all_gather(shard, "batch", axis=1, tiled=True),
            preferred_element_type=jnp.float32,
        )

    cond_act = jax.nn.silu(condition[0]).astype(jnp.bfloat16)
    cond_all = lax.all_gather(cond_act, "batch", axis=0, tiled=True)
    cond_cols = lax.dynamic_slice_in_dim(cond_all, batch_at * width_piece, width_piece, 1)
    block_local = jnp.transpose(modulation_weight, (1, 0, 2, 3)).reshape(
        width_piece, 6 * layer_count * head_cols
    )
    mod_local = jnp.concatenate(
        [block_local, final_modulation.reshape(width_piece, 2 * head_cols)], axis=1
    )
    mod_mine = lax.psum_scatter(
        jnp.dot(cond_cols, mod_local, preferred_element_type=jnp.float32),
        "batch",
        scatter_dimension=0,
        tiled=True,
    )
    mod_full = lax.all_gather(
        mod_mine.reshape(req_local, mod_count, head_cols), "tensor", axis=2, tiled=True
    )
    positions = jnp.arange(max_len, dtype=jnp.int32)
    live_mask = positions[None, :] < lengths[:, None]
    own_start = tensor_at * rows_local
    own_latents = lax.dynamic_slice_in_dim(latents, own_start, rows_local, 2)
    own_live = lax.dynamic_slice_in_dim(live_mask, own_start, rows_local, 1)
    hidden_state = (
        jnp.einsum("rpl,pd->rld", latents, embed_weight, precision=lax.Precision.HIGHEST)
        + position_table(max_len, width)[None]
    )
    for layer_at in range(layer_count):
        modulation = mod_full[:, 6 * layer_at : 6 * layer_at + 6]
        normed = modulate(hidden_state, modulation[:, 0], modulation[:, 1]).astype(jnp.bfloat16)
        projected = rows_product(
            normed.reshape(req_local * max_len, width),
            qkv_weight[layer_at].reshape(width_piece, 3 * head_cols),
        ).astype(jnp.bfloat16)
        projected = projected.reshape(req_local, max_len, 3, heads_local, HDIM)
        attended = lax.map(attend, (projected, live_mask))
        branch = cols_product(
            attended.reshape(req_local * max_len, head_cols), proj_weight[layer_at]
        ).reshape(req_local, max_len, width)
        branch = lax.psum(branch.astype(jnp.bfloat16), "tensor").astype(jnp.float32)
        hidden_state = hidden_state + modulation[:, 2][:, None, :] * branch
        normed = modulate(hidden_state, modulation[:, 3], modulation[:, 4]).astype(jnp.bfloat16)
        hidden_units = jax.nn.gelu(
            rows_product(normed.reshape(req_local * max_len, width), up_weight[layer_at]),
            approximate=True,
        ).astype(jnp.bfloat16)
        branch = cols_product(hidden_units, down_weight[layer_at]).reshape(
            req_local, max_len, width
        )
        branch = lax.psum(branch.astype(jnp.bfloat16), "tensor").astype(jnp.float32)
        hidden_state = hidden_state + modulation[:, 5][:, None, :] * branch
    hidden_state = lax.dynamic_slice_in_dim(hidden_state, own_start, rows_local, 1)
    final_in = modulate(
        hidden_state, mod_full[:, 6 * layer_count], mod_full[:, 6 * layer_count + 1]
    ).astype(jnp.bfloat16)
    noise_own = jnp.einsum(
        "rld,dp->rpl", final_in, output_weight, preferred_element_type=jnp.float32
    )
    half_patch = patch_size // 2
    mine_noise = lax.dynamic_slice_in_dim(noise_own, guide_at * half_patch, half_patch, 1)
    other_noise = lax.dynamic_slice_in_dim(noise_own, (1 - guide_at) * half_patch, half_patch, 1)
    partner_noise = from_partner(other_noise, "guide", 0)
    cond_noise = jnp.where(is_first, mine_noise, partner_noise)
    uncond_noise = jnp.where(is_first, partner_noise, mine_noise)
    live_out = own_live[:, None, :]
    guided = uncond_noise + guidance[:, None, None] * (cond_noise - uncond_noise)
    guided = jnp.where(live_out, guided, 0.0)
    half_latents = lax.dynamic_slice_in_dim(own_latents, guide_at * half_patch, half_patch, 1)
    beta_values = jnp.linspace(0.0001, 0.02, TRAIN_STEPS, dtype=jnp.float32)
    alpha_bar = jnp.cumprod(1.0 - beta_values)
    step_ids = jnp.arange(TRAIN_STEPS, dtype=jnp.int32)
    alpha_now = jnp.sum(
        jnp.where(step_ids[None, :] == timesteps[:, None], alpha_bar[None, :], 0.0), axis=1
    )[:, None, None]
    alpha_prev = jnp.sum(
        jnp.where(step_ids[None, :] == (timesteps - STRIDE)[:, None], alpha_bar[None, :], 0.0),
        axis=1,
    )[:, None, None]
    start_est = (half_latents - jnp.sqrt(1.0 - alpha_now) * guided) / jnp.sqrt(alpha_now)
    previous = jnp.sqrt(alpha_prev) * start_est + jnp.sqrt(1.0 - alpha_prev) * guided
    previous = jnp.where(live_out, previous, 0.0)
    return (guided, previous)


def solution(mesh):
    in_specs = (
        P("batch", None, None),
        P("batch"),
        P("batch"),
        P("batch"),
        P("guide", "batch", None),
        P(),
        P(None, "batch", None, "tensor"),
        P("batch", None, "tensor"),
        P(None, "batch", None, "tensor"),
        P(None, "tensor", "batch"),
        P(None, "batch", "tensor"),
        P(None, "tensor", "batch"),
        P(),
    )
    out_specs = (P("batch", "guide", "tensor"), P("batch", "guide", "tensor"))
    return jax.shard_map(local, mesh=mesh, in_specs=in_specs, out_specs=out_specs, check_vma=False)
```

profile of v0, /device:TPU:1, one launch (start us, length us, event | category | flops | bytes accessed | tf_op | source)
XLA Modules:
  0.0 909.3 jit_solution(10363798787262294825)
XLA Ops:
  7.2 0.7 fusion.119
  7.9 25.4 %all-gather.6 = bf16[8,1,1152]{2,1,0:T(2,128)(2,1)S(1)} all-gather(bf16[1,1,1152]{2,1,0:T(2,128)(2,1)S(1)} %fusion.119), channel_id=1, replica_groups=mesh['guide'=2,'tensor'=2,'batch'=8] {'batch'}, dimensions={0}, use_global_device_ids=true | all-gather | bytes 20736 | tf_op jit(solution)/shard_map/all_gather | solution.py:112
  33.3 2.2 copy.40
  35.6 3.2 reshape.338
  38.8 0.3 reshape.339
  39.2 2.7 fusion.58
  42.0 0.3 copy.42
  42.3 1.3 reshape_squeeze.6
  43.8 0.8 fusion.144
  44.6 4.1 multiply_sine_fusion
  48.7 2.1 fusion.145
  50.8 0.4 multiply_reduce_fusion.3
  51.9 0.6 dynamic-slice.11
  52.5 64.8 %all-reduce.16.cloned.1.call-done = f32[8,8064]{1,0:T(8,128)} async-done(((f32[8,8064]{1,0:T(8,128)}), f32[8,8064]{1,0:T(8,128)}) %all-reduce.16.cloned.1.call-update) | async-done | bytes 258064
  117.3 1.7 dynamic-slice_reduce_fusion
  119.2 6.8 all_gather.31
  126.0 62.0 %slice_reduce_fusion.2 = (f32[1152]{0:T(1024)S(1)}, f32[1152]{0:T(1024)S(1)}, f32[1152]{0:T(1024)S(1)}, f32[1152]{0:T(1024)S(1)}, f32[1152]{0:T(1024)S(1)}, /*in...) fusion(f32[1,14,1152]{1,0,2:T(1,128)S(1)} %all_gather.31), kind=kLoop, calls=%fused_computation.104 | loop fusion | flops 5760 | bytes 129024 | tf_op jit(solution)/shard_map/slice | solution.py:161
  188.0 4.9 all-gather.16.cloned.1.call-done
  192.9 5.8 convolution_convert_fusion.1
  198.7 3.0 copy.43
  201.7 5.9 fusion.146
  207.6 3.9 fusion.65
  211.5 26.3 %all-gather.20.cloned.1.call-done = bf16[1,576,1152]{1,2,0:T(8,128)(2,1)} async-done(((bf16[1,576,144]{1,2,0:T(8,128)(2,1)}), bf16[1,576,1152]{1,2,0:T(8,128)(2,1)}) %all-gather.20.cloned.1.call-update) | async-done | bytes 1327120 | tf_op jit(solution)/shard_map/all_gather | solution.py:107
  237.8 3.5 fusion.50
  241.4 1.2 fusion.141
  242.6 0.5 copy-done.7
  243.1 1.2 fusion.142
  244.3 35.8 %all-reduce.8.cloned.1.call-done = bf16[1,448,1152]{2,1,0:T(8,128)(2,1)} async-done(((bf16[1,448,1152]{2,1,0:T(8,128)(2,1)}), bf16[1,448,1152]{2,1,0:T(8,128)(2,1)}) %all-reduce.8.cloned.1.call-update) | async-done | bytes 1032208 | tf_op jit(solution)/shard_map/psum | solution.py:150
  280.1 2.2 fusion.140
  282.4 0.4 multiply_reduce_fusion.2
  282.8 85.9 %all-gather.22.cloned.1.call-done = bf16[1,1152,2304]{2,1,0:T(8,128)(2,1)} async-done(((bf16[1,144,2304]{2,1,0:T(8,128)(2,1)}), bf16[1,1152,2304]{2,1,0:T(8,128)(2,1)}) %all-gather.22.cloned.1.call-update) | async-done | bytes 5308432 | tf_op jit(solution)/shard_map/all_gather | solution.py:100
  368.6 87.5 %all-gather.24.cloned.1.call-done = bf16[1,2304,1152]{1,2,0:T(8,128)(2,1)} async-done(((bf16[1,2304,144]{1,2,0:T(8,128)(2,1)}), bf16[1,2304,1152]{1,2,0:T(8,128)(2,1)}) %all-gather.24.cloned.1.call-update) | async-done | bytes 5308432 | tf_op jit(solution)/shard_map/all_gather | solution.py:107
  456.2 10.9 %fusion.55 = bf16[1,448,1152]{2,1,0:T(8,128)(2,1)} fusion(bf16[1,2304,1152]{1,2,0:T(8,128)(2,1)} %all-gather.24.cloned.1.call-done, bf16[1,1152,2304]{2,1,0:T(8,128)(2,1)} %all-gather.22.cloned.1.call-done, f32[1,448,1152]{2,1,0:T(8,128)S(1)} %get-tuple-element.47, f32[1152]{0:T(1024)S(1)} %get-tuple-element.34, f32[1152]{0:T(1024)S(1)} %get-tuple-element.35, ...), kind=kOutput, calls=%fused_computation.54 | convolution fusion | flops 4768727040 | bytes 13726208 | tf_op jit(solution)/shard_map/dot_general | solution.py:105
  467.2 0.3 copy.45
  467.5 1.2 reshape_squeeze.7
  468.8 0.7 all-gather.26.cloned.1.call-update
  469.7 36.3 %all-reduce.10.cloned.1.call-done = bf16[1,448,1152]{2,1,0:T(8,128)(2,1)} async-done(((bf16[1,448,1152]{2,1,0:T(8,128)(2,1)}), bf16[1,448,1152]{2,1,0:T(8,128)(2,1)}) %all-reduce.10.cloned.1.call-update) | async-done | bytes 1032208 | tf_op jit(solution)/shard_map/psum | solution.py:160
  506.0 1.7 fusion.137
  507.7 0.5 multiply_reduce_fusion.1
  508.2 71.6 %all-gather.18.cloned.1.call-done = bf16[1152,1728]{1,0:T(8,128)(2,1)} async-done(((bf16[144,1728]{1,0:T(8,128)(2,1)}), bf16[1152,1728]{1,0:T(8,128)(2,1)}) %all-gather.18.cloned.1.call-update) | async-done | bytes 3981328 | tf_op jit(solution)/shard_map/all_gather | solution.py:100
  579.8 6.0 convolution_convert_fusion
  585.8 3.7 copy.46
  589.5 7.2 fusion.147
  596.7 4.9 fusion.64
  601.6 23.1 %all-gather.26.cloned.1.call-done = bf16[1,576,1152]{1,2,0:T(8,128)(2,1)} async-done(((bf16[1,576,144]{1,2,0:T(8,128)(2,1)}), bf16[1,576,1152]{1,2,0:T(8,128)(2,1)}) %all-gather.26.cloned.1.call-update) | async-done | bytes 1327120 | tf_op jit(solution)/shard_map/all_gather | solution.py:107
  624.7 3.6 fusion.51
  628.4 0.7 all-gather.28.cloned.1.call-update
  629.1 0.5 all-gather.30.cloned.1.call-update
  629.6 0.3 all-reduce.14.cloned.1.call-start
  629.9 37.2 %all-reduce.12.cloned.1.call-done = bf16[1,448,1152]{2,1,0:T(8,128)(2,1)} async-done(((bf16[1,448,1152]{2,1,0:T(8,128)(2,1)}), bf16[1,448,1152]{2,1,0:T(8,128)(2,1)}) %all-reduce.12.cloned.1.call-update) | async-done | bytes 1032208 | tf_op jit(solution)/shard_map/psum | solution.py:150
  667.1 1.8 fusion.139
  669.0 1.3 copy-done.3
  670.3 0.4 multiply_reduce_fusion
  670.6 85.2 %all-gather.28.cloned.1.call-done = bf16[1,1152,2304]{2,1,0:T(8,128)(2,1)} async-done(((bf16[1,144,2304]{2,1,0:T(8,128)(2,1)}), bf16[1,1152,2304]{2,1,0:T(8,128)(2,1)}) %all-gather.28.cloned.1.call-update) | async-done | bytes 5308432 | tf_op jit(solution)/shard_map/all_gather | solution.py:100
  755.8 87.5 %all-gather.30.cloned.1.call-done = bf16[1,2304,1152]{1,2,0:T(8,128)(2,1)} async-done(((bf16[1,2304,144]{1,2,0:T(8,128)(2,1)}), bf16[1,2304,1152]{1,2,0:T(8,128)(2,1)}) %all-gather.30.cloned.1.call-update) | async-done | bytes 5308432 | tf_op jit(solution)/shard_map/all_gather | solution.py:107
  843.4 11.6 %fusion.52 = bf16[1,448,1152]{2,1,0:T(8,128)(2,1)} fusion(bf16[1,2304,1152]{1,2,0:T(8,128)(2,1)} %all-gather.30.cloned.1.call-done, bf16[1,1152,2304]{2,1,0:T(8,128)(2,1)} %all-gather.28.cloned.1.call-done, f32[1,448,1152]{2,1,0:T(8,128)} %copy-done.3, f32[1152]{0:T(1024)S(1)} %get-tuple-element.25, f32[1152]{0:T(1024)S(1)} %get-tuple-element.26, ...), kind=kOutput, calls=%fused_computation.53 | convolution fusion | flops 4768727040 | bytes 13726208 | tf_op jit(solution)/shard_map/dot_general | solution.py:105
  855.1 0.3 reduce-window.9
  856.4 37.5 %all-reduce.14.cloned.1.call-done = bf16[1,448,1152]{2,1,0:T(8,128)(2,1)} async-done(((bf16[1,448,1152]{2,1,0:T(8,128)(2,1)}), bf16[1,448,1152]{2,1,0:T(8,128)(2,1)}) %all-reduce.14.cloned.1.call-update) | async-done | bytes 1032208 | tf_op jit(solution)/shard_map/psum | solution.py:160
  893.9 1.4 fusion.111
  895.3 1.4 multiply_reduce_fusion.4
  896.7 0.4 fusion.100
  897.0 0.8 collective-permute-start
  897.8 0.7 select_reduce_fusion
  901.8 0.7 add_select_fusion
  (77 shorter events, 1.9 us)
Async XLA Ops:
  7.2 41.5 %copy-start = (f32[16,1152]{1,0:T(8,128)S(1)}, f32[16,1152]{1,0:T(8,128)}, u32[]{:S(2)}) copy-start(f32[16,1152]{1,0:T(8,128)} %param.18) | copy-start | bytes 221188
  7.2 110.1 %all-reduce.16.cloned.1.call-start = ((), (), s32[]{:S(2)}) async-start(), calls=%async_computation.12 | async-start | bytes 516096
  35.6 3.3 copy-start.10
  38.8 3.1 copy-start.8
  41.9 151.1 %all-gather.16.cloned.1.call-start = ((), (), s32[]{:S(2)}) async-start(), calls=%async_computation | async-start | bytes 4644864 | tf_op jit(solution)/shard_map/all_gather | solution.py:100
  42.0 1.7 copy-start.11
  43.7 5.0 copy-start.12
  43.7 194.1 %all-gather.20.cloned.1.call-start = ((), (), s32[]{:S(2)}) async-start(), calls=%async_computation.6 | async-start | bytes 1658880 | tf_op jit(solution)/shard_map/all_gather | solution.py:107
  44.5 235.6 %all-reduce.8.cloned.1.call-start = ((), (), s32[]{:S(2)}) async-start(), calls=%async_computation.1 | async-start | bytes 2064384 | tf_op jit(solution)/shard_map/psum | solution.py:150
  50.8 142.1 %copy-start.2 = (f32[448,1152]{1,0:T(8,128)}, f32[448,1152]{1,0:T(8,128)S(1)}, u32[]{:S(2)}) copy-start(f32[448,1152]{1,0:T(8,128)S(1)} %get-tuple-element.59) | copy-start | bytes 6193156
  50.8 1.1 copy-start.14
  237.8 3.6 copy-start.6
  241.3 1.8 copy-start.7
  241.3 127.3 %all-gather.22.cloned.1.call-start = ((), (), s32[]{:S(2)}) async-start(), calls=%async_computation.7 | async-start | bytes 5971968 | tf_op jit(solution)/shard_map/all_gather | solution.py:100
  242.6 213.6 %all-gather.24.cloned.1.call-start = ((), (), s32[]{:S(2)}) async-start(), calls=%async_computation.8 | async-start | bytes 5971968 | tf_op jit(solution)/shard_map/all_gather | solution.py:107
  244.3 261.7 %all-reduce.10.cloned.1.call-start = ((), (), s32[]{:S(2)}) async-start(), calls=%async_computation.2 | async-start | bytes 2064384 | tf_op jit(solution)/shard_map/psum | solution.py:160
  467.1 112.7 %all-gather.18.cloned.1.call-start = ((), (), s32[]{:S(2)}) async-start(), calls=%async_computation.3 | async-start | bytes 4644864 | tf_op jit(solution)/shard_map/all_gather | solution.py:100
  468.7 156.0 %all-gather.26.cloned.1.call-start = ((), (), s32[]{:S(2)}) async-start(), calls=%async_computation.9 | async-start | bytes 1658880 | tf_op jit(solution)/shard_map/all_gather | solution.py:107
  469.5 197.7 %all-reduce.12.cloned.1.call-start = ((), (), s32[]{:S(2)}) async-start(), calls=%async_computation.4 | async-start | bytes 2064384 | tf_op jit(solution)/shard_map/psum | solution.py:150
  506.0 1.7 copy-start.5
  628.3 127.5 %all-gather.28.cloned.1.call-start = ((), (), s32[]{:S(2)}) async-start(), calls=%async_computation.10 | async-start | bytes 5971968 | tf_op jit(solution)/shard_map/all_gather | solution.py:100
  629.1 214.3 %all-gather.30.cloned.1.call-start = ((), (), s32[]{:S(2)}) async-start(), calls=%async_computation.11 | async-start | bytes 5971968 | tf_op jit(solution)/shard_map/all_gather | solution.py:107
  629.6 264.3 %all-reduce.14.cloned.1.call-start = ((), (), s32[]{:S(2)}) async-start(), calls=%async_computation.5 | async-start | bytes 2064384 | tf_op jit(solution)/shard_map/psum | solution.py:160
  668.9 1.3 copy-start.3
  843.4 50.6 %copy-start.4 = (f32[1,448,1152]{2,1,0:T(8,128)S(1)}, f32[1,448,1152]{2,1,0:T(8,128)}, u32[]{:S(2)}) copy-start(f32[1,448,1152]{2,1,0:T(8,128)} %copy-done.3) | copy-start | bytes 6193156
  855.0 41.6 %copy-start.13 = (bf16[1152,16]{0,1:T(8,128)(2,1)S(1)}, bf16[1152,16]{0,1:T(8,128)(2,1)}, u32[]{:S(2)}) copy-start(bf16[1152,16]{0,1:T(8,128)(2,1)} %param.25) | copy-start | bytes 110596
  893.9 2.7 copy-start.9
  893.9 8.6 copy-start.1
  897.0 4.8 collective-permute-start
Sparse Core Ops, SparseCore 0:
  42.0 75.2 all-reduce.15
  119.7 73.1 all-gather.15
  195.3 42.4 all-gather.19
  241.5 38.6 all-reduce.7
  282.4 86.2 all-gather.21
  370.9 85.2 all-gather.23
  467.2 38.7 all-reduce.9
  508.4 71.3 all-gather.17
  582.2 42.4 all-gather.25
  628.4 38.6 all-reduce.11
  669.6 86.2 all-gather.27
  758.1 85.2 all-gather.29
  855.2 38.7 all-reduce.13
where the time goes:
time: 917 us; the launch traced here: 909 us
  waiting for transfers between devices  686 us (75%)
  other arithmetic  78.8 us (9%)
  matrix products  68.4 us (7%)
  blocking collectives  32.2 us (4%)
  local copies, waits for them, and re-layouts  23.4 us (3%)
  between operations  19.1 us (2%)
    all_gather x4, waiting for transfers between devices, rows_product(): lax.all_gather(shard, 'batch', axis=0, tiled=True)  248 us
    all_gather x4, waiting for transfers between devices, cols_product(): lax.all_gather(shard, 'batch', axis=1, tiled=True)  224 us
    psum x4, waiting for transfers between devices, local(): branch = lax.psum(branch.astype(jnp.bfloat16), 'tensor').astype(jnp.float32)  147 us
    unnamed x14, waiting for transfers between devices  66.8 us
    slice x1, other arithmetic, local(): hidden_state = hidden_state + modulation[:, 5][:, None, :] * branch  62 us
    dot_general x4, matrix products, cols_product(): jnp.dot(activation, lax.all_gather(shard, 'batch', axis=1, tiled=True), p...  29.7 us
    all_gather x1, blocking collectives, local(): cond_all = lax.all_gather(cond_act, 'batch', axis=0, tiled=True)  25.4 us
  transfers between devices with their start and end apart: 14, of which 13 were waited for; matrix products, arithmetic and copies ran while one was open for 14% of the time, Pallas kernels for 0%

commit v1 on v0

--- a/solution.py
+++ b/solution.py
@@ -8,6 +8,39 @@
 TRAIN_STEPS = 1000
 STRIDE = 20
 norm_epsilon = 1e-06
+
+
+def widths_work(vector):
+    step_out = lax.psum(1, "batch")
+    local_out = lax.axis_index("batch")
+    current_block, carry_out, opened = (step_out, local_out, vector.shape[1])
+    series = []
+    hop_no = 0
+    while hop_no < current_block:
+        series.append((hop_no, (hop_no + 1) % current_block))
+        hop_no = hop_no + 1
+    samples = []
+    hop_no = 0
+    while hop_no < current_block:
+        samples.append((hop_no, (hop_no - 1) % current_block))
+        hop_no += 1
+    m_next = jnp.zeros((*vector.shape[:1], current_block * opened, *vector.shape[2:]), vector.dtype)
+    m_next = lax.dynamic_update_slice_in_dim(m_next, vector, carry_out * opened, axis=1)
+    all_values = even = vector
+    b_now = current_block // 2
+    w = 1
+    while w < b_now + 1:
+        all_values = lax.ppermute(all_values, "batch", series)
+        m_next = lax.dynamic_update_slice_in_dim(
+            m_next, all_values, (carry_out - w) % current_block * opened, axis=1
+        )
+        if w < current_block - b_now:
+            even = lax.ppermute(even, perm=samples, axis_name="batch")
+            m_next = lax.dynamic_update_slice_in_dim(
+                m_next, even, (carry_out + w) % current_block * opened, axis=1
+            )
+        w = w + 1
+    return m_next
 
 
 def from_partner(block, axis, distance):
@@ -102,11 +135,7 @@
         )
 
     def cols_product(activation, shard):
-        return jnp.dot(
-            activation,
-            lax.all_gather(shard, "batch", axis=1, tiled=True),
-            preferred_element_type=jnp.float32,
-        )
+        return jnp.dot(activation, widths_work(shard), preferred_element_type=jnp.float32)
 
     cond_act = jax.nn.silu(condition[0]).astype(jnp.bfloat16)
     cond_all = lax.all_gather(cond_act, "batch", axis=0, tiled=True)

time: 917 us -> 776 us (0.85)
  waiting for transfers between devices: 686 us -> 431 us
  starting transfers between devices: 1.75 us -> 79.5 us
  local copies, waits for them, and re-layouts: 23.4 us -> 58.5 us
    all_gather x4 -> x0, waiting for transfers between devices: 224 us -> none  [cols_product(): lax.all_gather(shard, 'batch', axis=1, tiled=True)]
    ppermute x0 -> x28, waiting for transfers between devices: none -> 194 us  [the longest x16 149 us: widths_work(): all_values = lax.ppermute(all_values, 'batch', series)]
    all_gather x4, waiting for transfers between devices: 248 us -> 138 us  [rows_product(): lax.all_gather(shard, 'batch', axis=0, tiled=True)]
    psum x4, waiting for transfers between devices: 147 us -> 42.9 us  [local(): branch = lax.psum(branch.astype(jnp.bfloat16), 'tensor').astype(jnp.float32)]
    ppermute x0 -> x28, starting transfers between devices: none -> 78.4 us  [the longest x12 56.2 us: widths_work(): even = lax.ppermute(even, perm=samples, axis_name='batch')]
    dynamic_update_slice x0 -> x32, local copies, waits for them, and re-layouts: none -> 27.3 us  [the longest x16 13.7 us: widths_work(): lax.dynamic_update_slice_in_dim(m_next, all_values, (carry_out - w) % cur...]
    unnamed x14 -> x10, waiting for transfers between devices: 66.8 us -> 55.9 us
  transfers between devices with their start and end apart: 14 -> 38, of which waited for: 13 -> 27; matrix products, arithmetic and copies ran while one was open for 14% -> 16% of each run, Pallas kernels for 0% -> 0%
where the time goes in v1:
time: 776 us; the launch traced here: 767 us
  waiting for transfers between devices  431 us (56%)
  starting transfers between devices  79.5 us (10%)
  other arithmetic  78.8 us (10%)
  matrix products  67.4 us (9%)
  local copies, waits for them, and re-layouts  58.5 us (8%)
  blocking collectives  32.2 us (4%)
  between operations  19.4 us (2%)
    ppermute x16, waiting for transfers between devices, widths_work(): all_values = lax.ppermute(all_values, 'batch', series)  149 us
    all_gather x4, waiting for transfers between devices, rows_product(): lax.all_gather(shard, 'batch', axis=0, tiled=True)  138 us
    slice x1, other arithmetic, local(): hidden_state = hidden_state + modulation[:, 5][:, None, :] * branch  62 us
    ppermute x12, starting transfers between devices, widths_work(): even = lax.ppermute(even, perm=samples, axis_name='batch')  56.2 us
    unnamed x10, waiting for transfers between devices  55.9 us
    ppermute x12, waiting for transfers between devices, widths_work(): even = lax.ppermute(even, perm=samples, axis_name='batch')  45.2 us
    psum x4, waiting for transfers between devices, local(): branch = lax.psum(branch.astype(jnp.bfloat16), 'tensor').astype(jnp.float32)  42.9 us
    dot_general x4, matrix products, cols_product(): jnp.dot(activation, widths_work(shard), preferred_element_type=jnp.float32)  29.6 us
  transfers between devices with their start and end apart: 38, of which 27 were waited for; matrix products, arithmetic and copies ran while one was open for 16% of the time, Pallas kernels for 0%

profile of v1, /device:TPU:1, one launch (start us, length us, event | category | flops | bytes accessed | tf_op | source)
XLA Modules:
  0.0 767.2 jit_solution(8205802288422102891)
XLA Ops:
  7.9 25.4 %all-gather.2 = bf16[8,1,1152]{2,1,0:T(2,128)(2,1)S(1)} all-gather(bf16[1,1,1152]{2,1,0:T(2,128)(2,1)S(1)} %fusion.107), channel_id=1, replica_groups=mesh['guide'=2,'tensor'=2,'batch'=8] {'batch'}, dimensions={0}, use_global_device_ids=true | all-gather | bytes 20736 | tf_op jit(solution)/shard_map/all_gather | solution.py:141
  33.3 2.2 copy.40
  35.6 3.2 reshape.338
  39.2 2.7 fusion.44
  45.8 2.9 collective-permute-start.1
  48.7 4.1 multiply_sine_fusion
  52.8 2.1 fusion.129
  58.8 4.1 collective-permute-start.3
  64.3 55.1 %all-reduce.16.cloned.1.call-done = f32[8,8064]{1,0:T(8,128)} async-done(((f32[8,8064]{1,0:T(8,128)}), f32[8,8064]{1,0:T(8,128)}) %all-reduce.16.cloned.1.call-update) | async-done | bytes 258064
  119.4 1.7 dynamic-slice_reduce_fusion
  121.3 6.8 all_gather.19
  128.1 62.0 %slice_reduce_fusion.2 = (f32[1152]{0:T(1024)S(1)}, f32[1152]{0:T(1024)S(1)}, f32[1152]{0:T(1024)S(1)}, f32[1152]{0:T(1024)S(1)}, f32[1152]{0:T(1024)S(1)}, /*in...) fusion(f32[1,14,1152]{1,0,2:T(1,128)S(1)} %all_gather.19), kind=kLoop, calls=%fused_computation.100 | loop fusion | flops 5760 | bytes 129024 | tf_op jit(solution)/shard_map/slice | solution.py:190
  191.7 2.7 collective-permute-start.5
  194.3 1.6 constant_dynamic-update-slice_fusion.28
  200.3 5.6 collective-permute-done.6
  206.6 5.8 convolution_convert_fusion.1
  212.4 2.9 copy.43
  215.2 5.9 fusion.130
  221.2 3.9 fusion.49
  225.0 3.6 fusion.40
  231.3 4.2 collective-permute-start.8
  235.5 2.7 broadcast.230.clone.1
  239.1 20.7 %collective-permute-done.7 = bf16[2304,144]{0,1:T(8,128)(2,1)S(1)} collective-permute-done((bf16[2304,144]{0,1:T(8,128)(2,1)S(1)}, bf16[2304,144]{0,1:T(8,128)(2,1)S(1)}, u32[]{:S(2)}, u32[]{:S(2)}) %collective-permute-start.7) | collective-permute-done | bytes 663584 | tf_op jit(solution)/shard_map/ppermute | solution.py:33
  259.9 2.2 collective-permute-start.9
  262.1 14.2 %collective-permute-start.10 = (bf16[2304,144]{0,1:T(8,128)(2,1)S(1)}, bf16[2304,144]{0,1:T(8,128)(2,1)S(1)}, u32[]{:S(2)}, u32[]{:S(2)}) collective-permute-start(bf16[2304,144]{0,1:T(8,128)(2,1)S(1)} %collective-permute-done.8), channel_id=1, source_target_pairs={{0,7},{1,0},{2,1},{3,2},{4,3},{5,4},{6,5},{7,6},{8,15},{9,8},{10,9... | collective-permute-start | bytes 1990664 | tf_op jit(solution)/shard_map/ppermute | solution.py:38
  278.0 18.1 %collective-permute-done.9 = bf16[2304,144]{0,1:T(8,128)(2,1)S(1)} collective-permute-done((bf16[2304,144]{0,1:T(8,128)(2,1)S(1)}, bf16[2304,144]{0,1:T(8,128)(2,1)S(1)}, u32[]{:S(2)}, u32[]{:S(2)}) %collective-permute-start.9) | collective-permute-done | bytes 663584 | tf_op jit(solution)/shard_map/ppermute | solution.py:33
  296.1 2.3 collective-permute-start.11
  299.1 14.4 %collective-permute-start.12 = (bf16[2304,144]{0,1:T(8,128)(2,1)S(1)}, bf16[2304,144]{0,1:T(8,128)(2,1)S(1)}, u32[]{:S(2)}, u32[]{:S(2)}) collective-permute-start(bf16[2304,144]{0,1:T(8,128)(2,1)S(1)} %collective-permute-done.10), channel_id=1, source_target_pairs={{0,7},{1,0},{2,1},{3,2},{4,3},{5,4},{6,5},{7,6},{8,15},{9,8},{10,9... | collective-permute-start | bytes 1990664 | tf_op jit(solution)/shard_map/ppermute | solution.py:38
  315.3 10.1 %collective-permute-done.11 = bf16[2304,144]{0,1:T(8,128)(2,1)S(1)} collective-permute-done((bf16[2304,144]{0,1:T(8,128)(2,1)S(1)}, bf16[2304,144]{0,1:T(8,128)(2,1)S(1)}, u32[]{:S(2)}, u32[]{:S(2)}) %collective-permute-start.11) | collective-permute-done | bytes 663584 | tf_op jit(solution)/shard_map/ppermute | solution.py:33
  325.4 2.5 collective-permute-start.13
  330.7 13.5 %collective-permute-done.13 = bf16[2304,144]{0,1:T(8,128)(2,1)S(1)} collective-permute-done((bf16[2304,144]{0,1:T(8,128)(2,1)S(1)}, bf16[2304,144]{0,1:T(8,128)(2,1)S(1)}, u32[]{:S(2)}, u32[]{:S(2)}) %collective-permute-start.13) | collective-permute-done | bytes 663584 | tf_op jit(solution)/shard_map/ppermute | solution.py:33
  345.1 2.2 fusion.126
  347.7 40.9 %all-gather.12.cloned.1.call-done = bf16[1,1152,2304]{2,1,0:T(8,128)(2,1)} async-done(((bf16[1,144,2304]{2,1,0:T(8,128)(2,1)}), bf16[1,1152,2304]{2,1,0:T(8,128)(2,1)}) %all-gather.12.cloned.1.call-update) | async-done | bytes 5308432 | tf_op jit(solution)/shard_map/all_gather | solution.py:133
  388.6 10.9 %fusion.42 = bf16[1,448,1152]{2,1,0:T(8,128)(2,1)} fusion(bf16[2304,1152]{0,1:T(8,128)(2,1)} %constant_dynamic-update-slice_fusion.16, bf16[1,1152,2304]{2,1,0:T(8,128)(2,1)} %all-gather.12.cloned.1.call-done, f32[1,448,1152]{2,1,0:T(8,128)S(1)} %get-tuple-element.47, f32[1152]{0:T(1024)S(1)} %get-tuple-element.34, f32[1152]{0:T(1024)S(1)} %get-tuple-element.35, ...), kind=kOutput, calls=%fused_computation.49 | convolution fusion | flops 4768727040 | bytes 13726208 | tf_op jit(solution)/shard_map/dot_general | solution.py:138
  401.2 4.5 collective-permute-start.14
  407.7 5.7 collective-permute-done.14
  413.4 2.2 collective-permute-start.16
  416.3 2.0 collective-permute-start.17
  418.9 3.1 collective-permute-done.16
  422.0 2.4 collective-permute-start.18
  430.0 4.4 collective-permute-done.19
  437.2 3.7 all-reduce.10.cloned.1.call-done
  440.9 1.7 fusion.124
  443.1 71.5 %all-gather.10.cloned.1.call-done = bf16[1152,1728]{1,0:T(8,128)(2,1)} async-done(((bf16[144,1728]{1,0:T(8,128)(2,1)}), bf16[1152,1728]{1,0:T(8,128)(2,1)}) %all-gather.10.cloned.1.call-update) | async-done | bytes 3981328 | tf_op jit(solution)/shard_map/all_gather | solution.py:133
  514.6 6.0 convolution_convert_fusion
  520.6 3.7 copy.46
  524.3 7.2 fusion.131
  531.5 4.1 fusion.48
  535.5 3.5 fusion.41
  540.2 3.9 collective-permute-start.22
  544.0 2.7 broadcast.230.clone
  547.7 19.4 %collective-permute-done.21 = bf16[2304,144]{0,1:T(8,128)(2,1)S(1)} collective-permute-done((bf16[2304,144]{0,1:T(8,128)(2,1)}, bf16[2304,144]{0,1:T(8,128)(2,1)S(1)}, u32[]{:S(2)}, u32[]{:S(2)}) %collective-permute-start.21) | collective-permute-done | bytes 663584 | tf_op jit(solution)/shard_map/ppermute | solution.py:33
  567.1 2.2 collective-permute-start.23
  569.5 3.4 collective-permute-start.24
  574.6 12.0 %collective-permute-done.23 = bf16[2304,144]{0,1:T(8,128)(2,1)S(1)} collective-permute-done((bf16[2304,144]{0,1:T(8,128)(2,1)S(1)}, bf16[2304,144]{0,1:T(8,128)(2,1)S(1)}, u32[]{:S(2)}, u32[]{:S(2)}) %collective-permute-start.23) | collective-permute-done | bytes 663584 | tf_op jit(solution)/shard_map/ppermute | solution.py:33
  586.7 18.4 %collective-permute-done.24 = bf16[2304,144]{0,1:T(8,128)(2,1)S(1)} collective-permute-done((bf16[2304,144]{0,1:T(8,128)(2,1)S(1)}, bf16[2304,144]{0,1:T(8,128)(2,1)S(1)}, u32[]{:S(2)}, u32[]{:S(2)}) %collective-permute-start.24) | collective-permute-done | bytes 663584 | tf_op jit(solution)/shard_map/ppermute | solution.py:38
  605.1 4.2 collective-permute-start.26
  611.1 21.5 %collective-permute-done.25 = bf16[2304,144]{0,1:T(8,128)(2,1)S(1)} collective-permute-done((bf16[2304,144]{0,1:T(8,128)(2,1)S(1)}, bf16[2304,144]{0,1:T(8,128)(2,1)S(1)}, u32[]{:S(2)}, u32[]{:S(2)}) %collective-permute-start.25) | collective-permute-done | bytes 663584 | tf_op jit(solution)/shard_map/ppermute | solution.py:33
  633.9 19.1 %collective-permute-done.26 = bf16[2304,144]{0,1:T(8,128)(2,1)S(1)} collective-permute-done((bf16[2304,144]{0,1:T(8,128)(2,1)S(1)}, bf16[2304,144]{0,1:T(8,128)(2,1)S(1)}, u32[]{:S(2)}, u32[]{:S(2)}) %collective-permute-start.26) | collective-permute-done | bytes 663584 | tf_op jit(solution)/shard_map/ppermute | solution.py:38
  653.8 15.2 %collective-permute-done.27 = bf16[2304,144]{0,1:T(8,128)(2,1)S(1)} collective-permute-done((bf16[2304,144]{0,1:T(8,128)(2,1)S(1)}, bf16[2304,144]{0,1:T(8,128)(2,1)S(1)}, u32[]{:S(2)}, u32[]{:S(2)}) %collective-permute-start.27) | collective-permute-done | bytes 663584 | tf_op jit(solution)/shard_map/ppermute | solution.py:33
  669.9 1.8 fusion.125
  673.4 26.0 %all-gather.14.cloned.1.call-done = bf16[1,1152,2304]{2,1,0:T(8,128)(2,1)} async-done(((bf16[1,144,2304]{2,1,0:T(8,128)(2,1)}), bf16[1,1152,2304]{2,1,0:T(8,128)(2,1)}) %all-gather.14.cloned.1.call-update) | async-done | bytes 5308432 | tf_op jit(solution)/shard_map/all_gather | solution.py:133
  699.4 11.6 %fusion.43 = bf16[1,448,1152]{2,1,0:T(8,128)(2,1)} fusion(bf16[2304,1152]{0,1:T(8,128)(2,1)} %constant_dynamic-update-slice_fusion, bf16[1,1152,2304]{2,1,0:T(8,128)(2,1)} %all-gather.14.cloned.1.call-done, f32[1,448,1152]{2,1,0:T(8,128)} %copy-done.3, f32[1152]{0:T(1024)S(1)} %get-tuple-element.25, f32[1152]{0:T(1024)S(1)} %get-tuple-element.26, ...), kind=kOutput, calls=%fused_computation.50 | convolution fusion | flops 4768727040 | bytes 13726208 | tf_op jit(solution)/shard_map/dot_general | solution.py:138
  712.4 39.2 %all-reduce.14.cloned.1.call-done = bf16[1,448,1152]{2,1,0:T(8,128)(2,1)} async-done(((bf16[1,448,1152]{2,1,0:T(8,128)(2,1)}), bf16[1,448,1152]{2,1,0:T(8,128)(2,1)}) %all-reduce.14.cloned.1.call-update) | async-done | bytes 1032208 | tf_op jit(solution)/shard_map/psum | solution.py:189
  (161 shorter events, 58.7 us)
Async XLA Ops:
  7.2 45.6 %copy-start = (f32[16,1152]{1,0:T(8,128)S(1)}, f32[16,1152]{1,0:T(8,128)}, u32[]{:S(2)}) copy-start(f32[16,1152]{1,0:T(8,128)} %param.18) | copy-start | bytes 221188
  7.2 112.2 %all-reduce.16.cloned.1.call-start = ((), (), s32[]{:S(2)}) async-start(), calls=%async_computation.8 | async-start | bytes 516096
  35.6 3.3 copy-start.13
  38.8 3.1 copy-start.11
  41.9 164.8 %all-gather.8.cloned.1.call-start = ((), (), s32[]{:S(2)}) async-start(), calls=%async_computation | async-start | bytes 4644864 | tf_op jit(solution)/shard_map/all_gather | solution.py:133
  42.0 1.7 copy-start.8
  43.7 9.1 %copy-start.14 = (f32[1,16,448]{2,1,0:T(8,128)S(1)}, f32[1,16,448]{2,1,0:T(8,128)}, u32[]{:S(2)}) copy-start(f32[1,16,448]{2,1,0:T(8,128)} %param.13) | copy-start | bytes 86020
  43.7 301.4 %all-reduce.8.cloned.1.call-start = ((), (), s32[]{:S(2)}) async-start(), calls=%async_computation.1 | async-start | bytes 2064384 | tf_op jit(solution)/shard_map/psum | solution.py:179
  44.5 14.2 %collective-permute-start = (bf16[576,144]{0,1:T(8,128)(2,1)}, bf16[576,144]{0,1:T(8,128)(2,1)S(1)}, u32[]{:S(2)}, u32[]{:S(2)}) collective-permute-start(bf16[576,144]{0,1:T(8,128)(2,1)} %get-tuple-element.55), channel_id=1, source_target_pairs={{0,1},{1,2},{2,3},{3,4},{4,5},{5,6},{6,7},{7,0},{8,9},{9,10},{10,1... | collective-permute-start | bytes 497672 | tf_op jit(solution)/shard_map/ppermute | solution.py:33
  45.8 12.9 %collective-permute-start.1 = (bf16[576,144]{0,1:T(8,128)(2,1)}, bf16[576,144]{0,1:T(8,128)(2,1)S(1)}, u32[]{:S(2)}, u32[]{:S(2)}) collective-permute-start(bf16[576,144]{0,1:T(8,128)(2,1)} %get-tuple-element.55), channel_id=1, source_target_pairs={{0,7},{1,0},{2,1},{3,2},{4,3},{5,4},{6,5},{7,6},{8,15},{9,8},{10,9... | collective-permute-start | bytes 497672 | tf_op jit(solution)/shard_map/ppermute | solution.py:38
  54.9 151.7 %copy-start.2 = (f32[448,1152]{1,0:T(8,128)}, f32[448,1152]{1,0:T(8,128)S(1)}, u32[]{:S(2)}) copy-start(f32[448,1152]{1,0:T(8,128)S(1)} %get-tuple-element.59) | copy-start | bytes 6193156
  54.9 3.2 copy-start.16
  58.7 131.4 %collective-permute-start.2 = (bf16[576,144]{0,1:T(8,128)(2,1)S(1)}, bf16[576,144]{0,1:T(8,128)(2,1)}, u32[]{:S(2)}, u32[]{:S(2)}) collective-permute-start(bf16[576,144]{0,1:T(8,128)(2,1)S(1)} %collective-permute-done), channel_id=1, source_target_pairs={{0,1},{1,2},{2,3},{3,4},{4,5},{5,6},{6,7},{7,0},{8,9},{9,10},{10,1... | collective-permute-start | bytes 497672 | tf_op jit(solution)/shard_map/ppermute | solution.py:33
  58.8 132.9 %collective-permute-start.3 = (bf16[576,144]{0,1:T(8,128)(2,1)S(1)}, bf16[576,144]{0,1:T(8,128)(2,1)}, u32[]{:S(2)}, u32[]{:S(2)}) collective-permute-start(bf16[576,144]{0,1:T(8,128)(2,1)S(1)} %collective-permute-done.1), channel_id=1, source_target_pairs={{0,7},{1,0},{2,1},{3,2},{4,3},{5,4},{6,5},{7,6},{8,15},{9,8},{10,9... | collective-permute-start | bytes 497672 | tf_op jit(solution)/shard_map/ppermute | solution.py:38
  190.1 8.6 %collective-permute-start.4 = (bf16[576,144]{0,1:T(8,128)(2,1)}, bf16[576,144]{0,1:T(8,128)(2,1)S(1)}, u32[]{:S(2)}, u32[]{:S(2)}) collective-permute-start(bf16[576,144]{0,1:T(8,128)(2,1)} %collective-permute-done.2), channel_id=1, source_target_pairs={{0,1},{1,2},{2,3},{3,4},{4,5},{5,6},{6,7},{7,0},{8,9},{9,10},{10,1... | collective-permute-start | bytes 497672 | tf_op jit(solution)/shard_map/ppermute | solution.py:33
  191.7 7.9 %collective-permute-start.5 = (bf16[576,144]{0,1:T(8,128)(2,1)}, bf16[576,144]{0,1:T(8,128)(2,1)S(1)}, u32[]{:S(2)}, u32[]{:S(2)}) collective-permute-start(bf16[576,144]{0,1:T(8,128)(2,1)} %collective-permute-done.3), channel_id=1, source_target_pairs={{0,7},{1,0},{2,1},{3,2},{4,3},{5,4},{6,5},{7,6},{8,15},{9,8},{10,9... | collective-permute-start | bytes 497672 | tf_op jit(solution)/shard_map/ppermute | solution.py:38
  198.7 7.2 collective-permute-start.6
  225.0 3.6 copy-start.10
  228.6 1.8 copy-start.6
  228.6 160.0 %all-gather.12.cloned.1.call-start = ((), (), s32[]{:S(2)}) async-start(), calls=%async_computation.6 | async-start | bytes 5971968 | tf_op jit(solution)/shard_map/all_gather | solution.py:133
  229.9 211.0 %all-reduce.10.cloned.1.call-start = ((), (), s32[]{:S(2)}) async-start(), calls=%async_computation.2 | async-start | bytes 2064384 | tf_op jit(solution)/shard_map/psum | solution.py:189
  231.3 28.5 %collective-permute-start.7 = (bf16[2304,144]{0,1:T(8,128)(2,1)S(1)}, bf16[2304,144]{0,1:T(8,128)(2,1)S(1)}, u32[]{:S(2)}, u32[]{:S(2)}) collective-permute-start(bf16[2304,144]{0,1:T(8,128)(2,1)S(1)} %get-tuple-element.50), channel_id=1, source_target_pairs={{0,1},{1,2},{2,3},{3,4},{4,5},{5,6},{6,7},{7,0},{8,9},{9,10},{10,1... | collective-permute-start | bytes 1990664 | tf_op jit(solution)/shard_map/ppermute | solution.py:33
  231.3 30.7 %collective-permute-start.8 = (bf16[2304,144]{0,1:T(8,128)(2,1)S(1)}, bf16[2304,144]{0,1:T(8,128)(2,1)S(1)}, u32[]{:S(2)}, u32[]{:S(2)}) collective-permute-start(bf16[2304,144]{0,1:T(8,128)(2,1)S(1)} %get-tuple-element.50), channel_id=1, source_target_pairs={{0,7},{1,0},{2,1},{3,2},{4,3},{5,4},{6,5},{7,6},{8,15},{9,8},{10,9... | collective-permute-start | bytes 1990664 | tf_op jit(solution)/shard_map/ppermute | solution.py:38
  259.9 36.3 %collective-permute-start.9 = (bf16[2304,144]{0,1:T(8,128)(2,1)S(1)}, bf16[2304,144]{0,1:T(8,128)(2,1)S(1)}, u32[]{:S(2)}, u32[]{:S(2)}) collective-permute-start(bf16[2304,144]{0,1:T(8,128)(2,1)S(1)} %collective-permute-done.7), channel_id=1, source_target_pairs={{0,1},{1,2},{2,3},{3,4},{4,5},{5,6},{6,7},{7,0},{8,9},{9,10},{10,1... | collective-permute-start | bytes 1990664 | tf_op jit(solution)/shard_map/ppermute | solution.py:33
  262.1 37.0 %collective-permute-start.10 = (bf16[2304,144]{0,1:T(8,128)(2,1)S(1)}, bf16[2304,144]{0,1:T(8,128)(2,1)S(1)}, u32[]{:S(2)}, u32[]{:S(2)}) collective-permute-start(bf16[2304,144]{0,1:T(8,128)(2,1)S(1)} %collective-permute-done.8), channel_id=1, source_target_pairs={{0,7},{1,0},{2,1},{3,2},{4,3},{5,4},{6,5},{7,6},{8,15},{9,8},{10,9... | collective-permute-start | bytes 1990664 | tf_op jit(solution)/shard_map/ppermute | solution.py:38
  296.1 29.2 %collective-permute-start.11 = (bf16[2304,144]{0,1:T(8,128)(2,1)S(1)}, bf16[2304,144]{0,1:T(8,128)(2,1)S(1)}, u32[]{:S(2)}, u32[]{:S(2)}) collective-permute-start(bf16[2304,144]{0,1:T(8,128)(2,1)S(1)} %collective-permute-done.9), channel_id=1, source_target_pairs={{0,1},{1,2},{2,3},{3,4},{4,5},{5,6},{6,7},{7,0},{8,9},{9,10},{10,1... | collective-permute-start | bytes 1990664 | tf_op jit(solution)/shard_map/ppermute | solution.py:33
  299.1 30.7 %collective-permute-start.12 = (bf16[2304,144]{0,1:T(8,128)(2,1)S(1)}, bf16[2304,144]{0,1:T(8,128)(2,1)S(1)}, u32[]{:S(2)}, u32[]{:S(2)}) collective-permute-start(bf16[2304,144]{0,1:T(8,128)(2,1)S(1)} %collective-permute-done.10), channel_id=1, source_target_pairs={{0,7},{1,0},{2,1},{3,2},{4,3},{5,4},{6,5},{7,6},{8,15},{9,8},{10,9... | collective-permute-start | bytes 1990664 | tf_op jit(solution)/shard_map/ppermute | solution.py:38
  325.4 18.7 %collective-permute-start.13 = (bf16[2304,144]{0,1:T(8,128)(2,1)S(1)}, bf16[2304,144]{0,1:T(8,128)(2,1)S(1)}, u32[]{:S(2)}, u32[]{:S(2)}) collective-permute-start(bf16[2304,144]{0,1:T(8,128)(2,1)S(1)} %collective-permute-done.11), channel_id=1, source_target_pairs={{0,1},{1,2},{2,3},{3,4},{4,5},{5,6},{6,7},{7,0},{8,9},{9,10},{10,1... | collective-permute-start | bytes 1990664 | tf_op jit(solution)/shard_map/ppermute | solution.py:33
  399.5 115.1 %all-gather.10.cloned.1.call-start = ((), (), s32[]{:S(2)}) async-start(), calls=%async_computation.3 | async-start | bytes 4644864 | tf_op jit(solution)/shard_map/all_gather | solution.py:133
  399.9 7.1 copy-start.9
  401.2 268.8 %all-reduce.12.cloned.1.call-start = ((), (), s32[]{:S(2)}) async-start(), calls=%async_computation.4 | async-start | bytes 2064384 | tf_op jit(solution)/shard_map/psum | solution.py:179
  401.2 12.2 %collective-permute-start.14 = (bf16[576,144]{0,1:T(8,128)(2,1)}, bf16[576,144]{0,1:T(8,128)(2,1)S(1)}, u32[]{:S(2)}, u32[]{:S(2)}) collective-permute-start(bf16[576,144]{0,1:T(8,128)(2,1)} %get-tuple-element.54), channel_id=1, source_target_pairs={{0,1},{1,2},{2,3},{3,4},{4,5},{5,6},{6,7},{7,0},{8,9},{9,10},{10,1... | collective-permute-start | bytes 497672 | tf_op jit(solution)/shard_map/ppermute | solution.py:33
  405.8 10.5 %collective-permute-start.15 = (bf16[576,144]{0,1:T(8,128)(2,1)}, bf16[576,144]{0,1:T(8,128)(2,1)S(1)}, u32[]{:S(2)}, u32[]{:S(2)}) collective-permute-start(bf16[576,144]{0,1:T(8,128)(2,1)} %get-tuple-element.54), channel_id=1, source_target_pairs={{0,7},{1,0},{2,1},{3,2},{4,3},{5,4},{6,5},{7,6},{8,15},{9,8},{10,9... | collective-permute-start | bytes 497672 | tf_op jit(solution)/shard_map/ppermute | solution.py:38
  413.4 8.6 %collective-permute-start.16 = (bf16[576,144]{0,1:T(8,128)(2,1)S(1)}, bf16[576,144]{0,1:T(8,128)(2,1)S(1)}, u32[]{:S(2)}, u32[]{:S(2)}) collective-permute-start(bf16[576,144]{0,1:T(8,128)(2,1)S(1)} %collective-permute-done.14), channel_id=1, source_target_pairs={{0,1},{1,2},{2,3},{3,4},{4,5},{5,6},{6,7},{7,0},{8,9},{9,10},{10,1... | collective-permute-start | bytes 497672 | tf_op jit(solution)/shard_map/ppermute | solution.py:33
  416.3 10.3 %collective-permute-start.17 = (bf16[576,144]{0,1:T(8,128)(2,1)S(1)}, bf16[576,144]{0,1:T(8,128)(2,1)S(1)}, u32[]{:S(2)}, u32[]{:S(2)}) collective-permute-start(bf16[576,144]{0,1:T(8,128)(2,1)S(1)} %collective-permute-done.15), channel_id=1, source_target_pairs={{0,7},{1,0},{2,1},{3,2},{4,3},{5,4},{6,5},{7,6},{8,15},{9,8},{10,9... | collective-permute-start | bytes 497672 | tf_op jit(solution)/shard_map/ppermute | solution.py:38
  422.0 7.1 collective-permute-start.18
  426.6 7.8 %collective-permute-start.19 = (bf16[576,144]{0,1:T(8,128)(2,1)S(1)}, bf16[576,144]{0,1:T(8,128)(2,1)S(1)}, u32[]{:S(2)}, u32[]{:S(2)}) collective-permute-start(bf16[576,144]{0,1:T(8,128)(2,1)S(1)} %collective-permute-done.17), channel_id=1, source_target_pairs={{0,7},{1,0},{2,1},{3,2},{4,3},{5,4},{6,5},{7,6},{8,15},{9,8},{10,9... | collective-permute-start | bytes 497672 | tf_op jit(solution)/shard_map/ppermute | solution.py:38
  429.1 7.4 collective-permute-start.20
  440.9 1.7 copy-start.5
  539.0 160.4 %all-gather.14.cloned.1.call-start = ((), (), s32[]{:S(2)}) async-start(), calls=%async_computation.7 | async-start | bytes 5971968 | tf_op jit(solution)/shard_map/all_gather | solution.py:133
  539.8 211.8 %all-reduce.14.cloned.1.call-start = ((), (), s32[]{:S(2)}) async-start(), calls=%async_computation.5 | async-start | bytes 2064384 | tf_op jit(solution)/shard_map/psum | solution.py:189
  539.8 6.9 copy-start.7
  539.8 27.2 %collective-permute-start.21 = (bf16[2304,144]{0,1:T(8,128)(2,1)}, bf16[2304,144]{0,1:T(8,128)(2,1)S(1)}, u32[]{:S(2)}, u32[]{:S(2)}) collective-permute-start(bf16[2304,144]{0,1:T(8,128)(2,1)} %get-tuple-element.51), channel_id=1, source_target_pairs={{0,1},{1,2},{2,3},{3,4},{4,5},{5,6},{6,7},{7,0},{8,9},{9,10},{10,1... | collective-permute-start | bytes 1990664 | tf_op jit(solution)/shard_map/ppermute | solution.py:33
  540.2 29.3 %collective-permute-start.22 = (bf16[2304,144]{0,1:T(8,128)(2,1)}, bf16[2304,144]{0,1:T(8,128)(2,1)S(1)}, u32[]{:S(2)}, u32[]{:S(2)}) collective-permute-start(bf16[2304,144]{0,1:T(8,128)(2,1)} %get-tuple-element.51), channel_id=1, source_target_pairs={{0,7},{1,0},{2,1},{3,2},{4,3},{5,4},{6,5},{7,6},{8,15},{9,8},{10,9... | collective-permute-start | bytes 1990664 | tf_op jit(solution)/shard_map/ppermute | solution.py:38
  567.1 19.6 %collective-permute-start.23 = (bf16[2304,144]{0,1:T(8,128)(2,1)S(1)}, bf16[2304,144]{0,1:T(8,128)(2,1)S(1)}, u32[]{:S(2)}, u32[]{:S(2)}) collective-permute-start(bf16[2304,144]{0,1:T(8,128)(2,1)S(1)} %collective-permute-done.21), channel_id=1, source_target_pairs={{0,1},{1,2},{2,3},{3,4},{4,5},{5,6},{6,7},{7,0},{8,9},{9,10},{10,1... | collective-permute-start | bytes 1990664 | tf_op jit(solution)/shard_map/ppermute | solution.py:33
  569.5 35.6 %collective-permute-start.24 = (bf16[2304,144]{0,1:T(8,128)(2,1)S(1)}, bf16[2304,144]{0,1:T(8,128)(2,1)S(1)}, u32[]{:S(2)}, u32[]{:S(2)}) collective-permute-start(bf16[2304,144]{0,1:T(8,128)(2,1)S(1)} %collective-permute-done.22), channel_id=1, source_target_pairs={{0,7},{1,0},{2,1},{3,2},{4,3},{5,4},{6,5},{7,6},{8,15},{9,8},{10,9... | collective-permute-start | bytes 1990664 | tf_op jit(solution)/shard_map/ppermute | solution.py:38
  586.7 46.0 %collective-permute-start.25 = (bf16[2304,144]{0,1:T(8,128)(2,1)S(1)}, bf16[2304,144]{0,1:T(8,128)(2,1)S(1)}, u32[]{:S(2)}, u32[]{:S(2)}) collective-permute-start(bf16[2304,144]{0,1:T(8,128)(2,1)S(1)} %collective-permute-done.23), channel_id=1, source_target_pairs={{0,1},{1,2},{2,3},{3,4},{4,5},{5,6},{6,7},{7,0},{8,9},{9,10},{10,1... | collective-permute-start | bytes 1990664 | tf_op jit(solution)/shard_map/ppermute | solution.py:33
  605.1 47.8 %collective-permute-start.26 = (bf16[2304,144]{0,1:T(8,128)(2,1)S(1)}, bf16[2304,144]{0,1:T(8,128)(2,1)S(1)}, u32[]{:S(2)}, u32[]{:S(2)}) collective-permute-start(bf16[2304,144]{0,1:T(8,128)(2,1)S(1)} %collective-permute-done.24), channel_id=1, source_target_pairs={{0,7},{1,0},{2,1},{3,2},{4,3},{5,4},{6,5},{7,6},{8,15},{9,8},{10,9... | collective-permute-start | bytes 1990664 | tf_op jit(solution)/shard_map/ppermute | solution.py:38
  632.6 36.4 %collective-permute-start.27 = (bf16[2304,144]{0,1:T(8,128)(2,1)S(1)}, bf16[2304,144]{0,1:T(8,128)(2,1)S(1)}, u32[]{:S(2)}, u32[]{:S(2)}) collective-permute-start(bf16[2304,144]{0,1:T(8,128)(2,1)S(1)} %collective-permute-done.25), channel_id=1, source_target_pairs={{0,1},{1,2},{2,3},{3,4},{4,5},{5,6},{6,7},{7,0},{8,9},{9,10},{10,1... | collective-permute-start | bytes 1990664 | tf_op jit(solution)/shard_map/ppermute | solution.py:33
  671.7 1.3 copy-start.3
  699.4 52.2 %copy-start.4 = (f32[1,448,1152]{2,1,0:T(8,128)S(1)}, f32[1,448,1152]{2,1,0:T(8,128)}, u32[]{:S(2)}) copy-start(f32[1,448,1152]{2,1,0:T(8,128)} %copy-done.3) | copy-start | bytes 6193156
  711.1 43.3 %copy-start.15 = (bf16[1152,16]{0,1:T(8,128)(2,1)S(1)}, bf16[1152,16]{0,1:T(8,128)(2,1)}, u32[]{:S(2)}) copy-start(bf16[1152,16]{0,1:T(8,128)(2,1)} %param.25) | copy-start | bytes 110596
  751.6 2.7 copy-start.12
  751.6 8.6 %copy-start.1 = (f32[16,1152]{1,0:T(8,128)S(1)}, f32[16,1152]{1,0:T(8,128)}, u32[]{:S(2)}) copy-start(f32[16,1152]{1,0:T(8,128)} %param.18) | copy-start | bytes 221188
  754.7 4.8 collective-permute-start.28
Sparse Core Ops, SparseCore 0:
  42.0 77.3 all-reduce.15
  121.8 73.1 all-gather.7
  228.7 43.8 all-reduce.7
  274.9 113.6 all-gather.11
  399.7 41.2 all-reduce.9
  443.2 71.3 all-gather.9
  539.1 39.1 all-reduce.11
  580.7 118.6 all-gather.13
  711.2 40.3 all-reduce.13
